TPU v7x, 512 devices: a whole 4x4x16 slice. The times are simulated.
512 devices in a mesh: pts: 16 (over z), elem: 32 (over y, x, core).
Axes of the slice: x: 4, y: 4, z: 16, core: 2. Of those that a mesh axis runs over, the one named last changes fastest.
Arguments:
- theta: float32 [1024, 1024], P('elem', 'pts'), may hold values from -3.140625 to 3.140625
- panel_rows: int32 [1024], P('elem'), may hold values from 0 to 1023, each once
- point_rows: int32 [32768], P('pts'), may hold values from 0 to 511
- point_cols: int32 [32768], P('pts'), may hold values from 0 to 255
- direct: float32 [2, 32768], P(None, 'pts'), may hold values from -3 to 3
- noise: float32 [32768], P('pts'), may hold values from 0.05 to 0.5
Outputs:
- phase_grad: float32 [1024, 1024], P('elem', 'pts')
- field: float32 [2, 32768], P(None, 'pts')
Inputs may be any that keep to these rules, and one draw needn't show every extreme that they name: `panel_rows`: each lattice row appears once.
All inputs are finite; a program needn't handle non-finite values.
Results may differ from a plain program's by a relative error of at most 0.0004.
Values sent between devices are 32-bit elements; how exact they have to be, the bound alone decides.
No kernel may reach another device: no remote copies, remote signals or barrier semaphores. Data moves between devices by JAX's collectives and lax.ppermute only.
A program may use at most 64 MiB of HBM per device.

v0:
```python
import math
import jax
import jax.numpy as jnp
from jax import lax
from jax.sharding import PartitionSpec as P

NX_EL = 1024
NY_EL = 1024
HIGH = lax.Precision.HIGHEST


def geometry(point_rows, point_cols):
    along_x = (point_rows.astype(jnp.float32) - 255.5) * 0.5
    along_y = (point_cols.astype(jnp.float32) - 127.5) * 0.5
    radius = jnp.sqrt(along_x * along_x + along_y * along_y + 1600.0)
    return (along_x / radius, along_y / radius, 80.0 / (radius * math.sqrt(NX_EL * NY_EL)))


def partial_field(slope_x, slope_y, lattice_x, lattice_y, phase_re, phase_im):
    beam_y = math.pi * slope_y[:, None] * lattice_y[None, :]
    left = jnp.concatenate([jnp.cos(beam_y), jnp.sin(beam_y)], 1)
    right = jnp.concatenate(
        [
            jnp.concatenate([phase_re.T, phase_im.T], 1),
            jnp.concatenate([-phase_im.T, phase_re.T], 1),
        ],
        0,
    )
    inner = jnp.dot(left, right, precision=HIGH, preferred_element_type=jnp.float32)
    width = phase_re.shape[0]
    inner_re = inner[:, :width]
    inner_im = inner[:, width:]
    beam_x = math.pi * slope_x[:, None] * lattice_x[None, :]
    cos_x = jnp.cos(beam_x)
    sin_x = jnp.sin(beam_x)
    return jnp.stack(
        [
            jnp.sum(cos_x * inner_re - sin_x * inner_im, 1),
            jnp.sum(cos_x * inner_im + sin_x * inner_re, 1),
        ]
    )


def surface_terms(slope_x, slope_y, q_re, q_im, lattice_x, lattice_y):
    beam_x = math.pi * slope_x[:, None] * lattice_x[None, :]
    cos_x = jnp.cos(beam_x)
    sin_x = jnp.sin(beam_x)
    weight_re = q_re[:, None] * cos_x - q_im[:, None] * sin_x
    weight_im = q_re[:, None] * sin_x + q_im[:, None] * cos_x
    beam_y = math.pi * slope_y[:, None] * lattice_y[None, :]
    left = jnp.concatenate([jnp.cos(beam_y), jnp.sin(beam_y)], 1)
    right = jnp.concatenate([weight_re, weight_im], 1)
    prod = lax.dot_general(
        left, right, (((0,), (0,)), ((), ())), precision=HIGH, preferred_element_type=jnp.float32
    )
    rows_y = lattice_y.shape[0]
    cols_x = lattice_x.shape[0]
    sum_re = prod[:rows_y, :cols_x] - prod[rows_y:, cols_x:]
    sum_im = prod[:rows_y, cols_x:] + prod[rows_y:, :cols_x]
    return jnp.concatenate([sum_re, sum_im], 1)


def block_size(points, cols_y):
    return math.gcd(points, min(points, max(256, 524288 // cols_y)))


def field_blocks(slope_x, slope_y, lattice_x, lattice_y, phase_re, phase_im):
    block = block_size(slope_x.shape[0], lattice_y.shape[0])
    count = slope_x.shape[0] // block

    def one_block(pair):
        return partial_field(pair[0], pair[1], lattice_x, lattice_y, phase_re, phase_im)

    parts = lax.map(one_block, (slope_x.reshape(count, block), slope_y.reshape(count, block)))
    return jnp.transpose(parts, (1, 0, 2)).reshape(2, count * block)


def terms_blocks(slope_x, slope_y, q_re, q_im, lattice_x, lattice_y):
    block = block_size(slope_x.shape[0], lattice_y.shape[0])
    count = slope_x.shape[0] // block
    start = jnp.zeros((lattice_y.shape[0], 2 * lattice_x.shape[0]), jnp.float32)

    def step(carry, items):
        return (
            carry + surface_terms(items[0], items[1], items[2], items[3], lattice_x, lattice_y),
            None,
        )

    items = (
        slope_x.reshape(count, block),
        slope_y.reshape(count, block),
        q_re.reshape(count, block),
        q_im.reshape(count, block),
    )
    total, unused = lax.scan(step, start, items)
    return total


def weights(field, scale, noise):
    power = noise + field[0] * field[0] + field[1] * field[1]
    return (field[0] * scale / power, -field[1] * scale / power)


def gradient(terms, phase_re, phase_im):
    cols_x = phase_re.shape[0]
    sum_re = terms[:, :cols_x].T
    sum_im = terms[:, cols_x:].T
    return -2.0 * (phase_re * sum_im + phase_im * sum_re)


def shards(theta, panel_rows, point_rows, point_cols, direct, noise):
    slope_x, slope_y, scale = geometry(point_rows, point_cols)
    phase_re = jnp.cos(theta)
    phase_im = jnp.sin(theta)
    lattice_x = panel_rows.astype(jnp.float32) - (NX_EL - 1) / 2.0
    cols_dev = theta.shape[1]
    phasors = jnp.stack([phase_re, phase_im])
    whole = lax.all_gather(phasors, "pts", axis=2, tiled=True)
    lattice_y = jnp.arange(NY_EL).astype(jnp.float32) - (NY_EL - 1) / 2.0
    partial_value = field_blocks(slope_x, slope_y, lattice_x, lattice_y, whole[0], whole[1])
    total = lax.psum(partial_value, "elem")
    field = direct + scale[None, :] * total
    q_re, q_im = weights(field, scale, noise)
    cols_here = jnp.arange(cols_dev * lax.axis_size("pts")).astype(jnp.float32) - (NY_EL - 1) / 2.0
    terms = lax.psum_scatter(
        terms_blocks(slope_x, slope_y, q_re, q_im, lattice_x, cols_here),
        "pts",
        scatter_dimension=0,
        tiled=True,
    )
    return (gradient(terms, phase_re, phase_im), field)


def solution(mesh):
    in_specs = (P("elem", "pts"), P("elem"), P("pts"), P("pts"), P(None, "pts"), P("pts"))
    out_specs = (P("elem", "pts"), P(None, "pts"))
    return jax.shard_map(shards, mesh=mesh, in_specs=in_specs, out_specs=out_specs, check_vma=False)
```

profile of v0, /device:TPU:2, one launch (start us, length us, event | category | flops | bytes accessed | tf_op | source)
XLA Modules:
  0.0 337.5 jit_solution(4195258781509086454)
XLA Ops:
  7.2 0.0 reduce-scatter.4.cloned.1.call-start
  7.2 0.8 copy.18
  8.0 0.1 fusion.39
  8.2 0.1 pad_maximum_fusion
  8.2 0.0 copy-start.2
  8.3 0.0 copy-start.5
  8.3 41.7 %all_gather.3 = f32[2,32,1024]{1,0,2:T(2,128)S(1)} all-gather(f32[2,32,64]{1,0,2:T(2,128)S(1)} %pad_maximum_fusion), channel_id=1, replica_groups=mesh['pts'=16,'elem'=32] {'pts'}, dimensions={2}, use_global_device_ids=true | all-gather | bytes 278528 | tf_op jit(solution)/shard_map/all_gather | solution.py:118
  49.9 0.8 fusion.38
  50.9 0.3 maximum_maximum_fusion
  51.2 0.0 copy-start.1
  51.3 47.9 %while.24 = (s32[]{:T(128)}, f32[4,2,512]{2,1,0:T(2,128)S(1)}, f32[4,512]{1,0:T(4,128)S(1)}, f32[32]{0:T(128)S(1)}, f32[4,512]{1,0:T(4,128)S(1)}, /*index=5*/f32[2048,64]{1,0:T(8,128)S(1)}, s32[]{:T(128)}) while((s32[]{:T(128)}, f32[4,2,512]{2,1,0:T(2,128)S(1)}, f32[4,512]{1,0:T(4,128)S(1)}, f32[32]{0:T(128)S(1)}, ...), condition=%wide.region_3.4_spmd.clone, body=%wide.region_0.3_spmd.clone.sunk | while | flops 807029760 | bytes 9208021 | solution.py:74
  51.3 7.3 %multiply_cosine_fusion.6 = (f32[512,1024]{1,0:T(8,128)S(1)}, f32[512,1024]{1,0:T(8,128)S(1)}) fusion(f32[1024]{0:T(1024)S(1)} %convert_add_fusion.5, f32[512]{0:T(512)S(1)} %bitcast.76), kind=kLoop, calls=%fused_computation.7.clone.1 | loop fusion | flops 524288 | bytes 4200448 | tf_op jit(solution)/shard_map/while/body/eval_jaxpr/cos | solution.py:21
  58.7 4.2 %fusion.52 = f32[512,64]{0,1:T(8,128)S(1)} fusion(f32[2048,64]{1,0:T(8,128)S(1)} %get-tuple-element.375, f32[512,1024]{1,0:T(8,128)S(1)} %get-tuple-element.334, f32[512,1024]{1,0:T(8,128)S(1)} %get-tuple-element.335), kind=kOutput, calls=%fused_computation.2.clone.1 | convolution fusion | flops 806354944 | bytes 4849664 | tf_op jit(solution)/shard_map/while/body/eval_jaxpr/dot_general | solution.py:29
  62.9 0.3 fusion.53
  63.3 7.3 %multiply_cosine_fusion.6 = (f32[512,1024]{1,0:T(8,128)S(1)}, f32[512,1024]{1,0:T(8,128)S(1)}) fusion(f32[1024]{0:T(1024)S(1)} %convert_add_fusion.5, f32[512]{0:T(512)S(1)} %bitcast.76), kind=kLoop, calls=%fused_computation.7.clone.1 | loop fusion | flops 524288 | bytes 4200448 | tf_op jit(solution)/shard_map/while/body/eval_jaxpr/cos | solution.py:21
  70.6 4.2 %fusion.52 = f32[512,64]{0,1:T(8,128)S(1)} fusion(f32[2048,64]{1,0:T(8,128)S(1)} %get-tuple-element.375, f32[512,1024]{1,0:T(8,128)S(1)} %get-tuple-element.334, f32[512,1024]{1,0:T(8,128)S(1)} %get-tuple-element.335), kind=kOutput, calls=%fused_computation.2.clone.1 | convolution fusion | flops 806354944 | bytes 4849664 | tf_op jit(solution)/shard_map/while/body/eval_jaxpr/dot_general | solution.py:29
  74.9 0.3 fusion.53
  75.3 7.3 %multiply_cosine_fusion.6 = (f32[512,1024]{1,0:T(8,128)S(1)}, f32[512,1024]{1,0:T(8,128)S(1)}) fusion(f32[1024]{0:T(1024)S(1)} %convert_add_fusion.5, f32[512]{0:T(512)S(1)} %bitcast.76), kind=kLoop, calls=%fused_computation.7.clone.1 | loop fusion | flops 524288 | bytes 4200448 | tf_op jit(solution)/shard_map/while/body/eval_jaxpr/cos | solution.py:21
  82.6 4.2 %fusion.52 = f32[512,64]{0,1:T(8,128)S(1)} fusion(f32[2048,64]{1,0:T(8,128)S(1)} %get-tuple-element.375, f32[512,1024]{1,0:T(8,128)S(1)} %get-tuple-element.334, f32[512,1024]{1,0:T(8,128)S(1)} %get-tuple-element.335), kind=kOutput, calls=%fused_computation.2.clone.1 | convolution fusion | flops 806354944 | bytes 4849664 | tf_op jit(solution)/shard_map/while/body/eval_jaxpr/dot_general | solution.py:29
  86.8 0.3 fusion.53
  87.2 7.3 %multiply_cosine_fusion.6 = (f32[512,1024]{1,0:T(8,128)S(1)}, f32[512,1024]{1,0:T(8,128)S(1)}) fusion(f32[1024]{0:T(1024)S(1)} %convert_add_fusion.5, f32[512]{0:T(512)S(1)} %bitcast.76), kind=kLoop, calls=%fused_computation.7.clone.1 | loop fusion | flops 524288 | bytes 4200448 | tf_op jit(solution)/shard_map/while/body/eval_jaxpr/cos | solution.py:21
  94.6 4.2 %fusion.52 = f32[512,64]{0,1:T(8,128)S(1)} fusion(f32[2048,64]{1,0:T(8,128)S(1)} %get-tuple-element.375, f32[512,1024]{1,0:T(8,128)S(1)} %get-tuple-element.334, f32[512,1024]{1,0:T(8,128)S(1)} %get-tuple-element.335), kind=kOutput, calls=%fused_computation.2.clone.1 | convolution fusion | flops 806354944 | bytes 4849664 | tf_op jit(solution)/shard_map/while/body/eval_jaxpr/dot_general | solution.py:29
  98.8 0.3 fusion.53
  99.2 119.2 %psum.7 = f32[2,2048]{1,0:T(2,128)S(1)} all-reduce(f32[2,2048]{1,0:T(2,128)S(1)} %bitcast.82), channel_id=1, replica_groups=mesh['pts'=16,'elem'=32] {'elem'}, use_global_device_ids=true, to_apply=%region_4.5 | all-reduce | flops 4096 | bytes 32768 | tf_op jit(solution)/shard_map/psum | solution.py:121
  218.4 0.0 copy-start
  218.4 0.5 copy-done
  219.0 42.9 %while.25 = (s32[]{:T(128)}, f32[1024,64]{0,1:T(8,128)S(1)}, f32[4,512]{1,0:T(4,128)S(1)}, f32[4,512]{1,0:T(4,128)S(1)}, f32[4,512]{1,0:T(4,128)S(1)}, /*index=5...) while((s32[]{:T(128)}, f32[1024,64]{0,1:T(8,128)S(1)}, f32[4,512]{1,0:T(4,128)S(1)}, ...), condition=%wide.region_6.7_spmd.clone, body=%wide.region_5.6_spmd.clone.sunk | while | flops 807291904 | bytes 10780911 | solution.py:95
  219.0 0.3 fusion.57
  219.3 7.3 %multiply_cosine_fusion.7 = (f32[512,1024]{1,0:T(8,128)S(1)}, f32[512,1024]{1,0:T(8,128)S(1)}) fusion(f32[1024]{0:T(1024)S(1)} %convert_add_fusion.6, f32[512]{0:T(512)S(1)} %bitcast.72), kind=kLoop, calls=%fused_computation.29.clone.1 | loop fusion | flops 524288 | bytes 4200448 | tf_op jit(solution)/shard_map/while/body/eval_jaxpr/cos | solution.py:51
  226.7 2.8 fusion.58
  229.6 0.1 maximum_add_fusion.2
  229.7 0.3 fusion.57
  230.1 7.3 %multiply_cosine_fusion.7 = (f32[512,1024]{1,0:T(8,128)S(1)}, f32[512,1024]{1,0:T(8,128)S(1)}) fusion(f32[1024]{0:T(1024)S(1)} %convert_add_fusion.6, f32[512]{0:T(512)S(1)} %bitcast.72), kind=kLoop, calls=%fused_computation.29.clone.1 | loop fusion | flops 524288 | bytes 4200448 | tf_op jit(solution)/shard_map/while/body/eval_jaxpr/cos | solution.py:51
  237.4 2.8 fusion.58
  240.3 0.1 maximum_add_fusion.2
  240.4 0.3 fusion.57
  240.8 7.3 %multiply_cosine_fusion.7 = (f32[512,1024]{1,0:T(8,128)S(1)}, f32[512,1024]{1,0:T(8,128)S(1)}) fusion(f32[1024]{0:T(1024)S(1)} %convert_add_fusion.6, f32[512]{0:T(512)S(1)} %bitcast.72), kind=kLoop, calls=%fused_computation.29.clone.1 | loop fusion | flops 524288 | bytes 4200448 | tf_op jit(solution)/shard_map/while/body/eval_jaxpr/cos | solution.py:51
  248.1 2.8 fusion.58
  251.0 0.1 maximum_add_fusion.2
  251.2 0.3 fusion.57
  251.5 7.3 %multiply_cosine_fusion.7 = (f32[512,1024]{1,0:T(8,128)S(1)}, f32[512,1024]{1,0:T(8,128)S(1)}) fusion(f32[1024]{0:T(1024)S(1)} %convert_add_fusion.6, f32[512]{0:T(512)S(1)} %bitcast.72), kind=kLoop, calls=%fused_computation.29.clone.1 | loop fusion | flops 524288 | bytes 4200448 | tf_op jit(solution)/shard_map/while/body/eval_jaxpr/cos | solution.py:51
  258.8 2.8 fusion.58
  261.7 0.1 maximum_add_fusion.2
  261.8 1.0 copy.26
  262.8 0.0 reduce-scatter.4.cloned.1.call-update
  262.9 66.2 %reduce-scatter.4.cloned.1.call-done = f32[64,64]{1,0:T(8,128)} async-done(((f32[1024,64]{1,0:T(8,128)}), f32[64,64]{1,0:T(8,128)}) %reduce-scatter.4.cloned.1.call-update) | async-done | bytes 16400 | tf_op jit(solution)/shard_map/reduce_scatter | solution.py:125
  329.1 0.9 fusion.34
  330.0 0.7 copy.25
  (47 shorter events, 0.5 us)
Async XLA Ops:
  7.2 321.9 %reduce-scatter.4.cloned.1.call-start = ((), (), s32[]{:S(2)}) async-start(), calls=%async_computation.1 | async-start | bytes 557056 | tf_op jit(solution)/shard_map/reduce_scatter | solution.py:125
  8.2 42.6 %copy-start.2 = (s32[2048]{0:T(1024)S(1)}, s32[2048]{0:T(1024)}, u32[]{:S(2)}) copy-start(s32[2048]{0:T(1024)} %param.13) | copy-start | bytes 24580
  8.3 42.6 %copy-start.3 = (s32[2048]{0:T(1024)S(1)}, s32[2048]{0:T(1024)}, u32[]{:S(2)}) copy-start(s32[2048]{0:T(1024)} %param.12) | copy-start | bytes 24580
  8.3 42.6 %copy-start.5 = (s32[32]{0:T(128)S(1)}, s32[32]{0:T(128)}, u32[]{:S(2)}) copy-start(s32[32]{0:T(128)} %param.11) | copy-start | bytes 388
  51.2 167.1 %copy-start.1 = (f32[2,2048]{1,0:T(2,128)S(1)}, f32[2,2048]{1,0:T(2,128)}, u32[]{:S(2)}) copy-start(f32[2,2048]{1,0:T(2,128)} %param.14) | copy-start | bytes 49156
  51.3 167.1 %copy-start.4 = (f32[2048]{0:T(1024)S(1)}, f32[2048]{0:T(1024)}, u32[]{:S(2)}) copy-start(f32[2048]{0:T(1024)} %param.15) | copy-start | bytes 24580
  218.4 0.6 copy-start
Sparse Core Ops, SparseCore 0:
  263.0 66.0 reduce-scatter.3
where the time goes:
time: 338 us
  blocking collectives  161 us (48%)
  waiting for transfers between devices  66.2 us (20%)
  other arithmetic  63.5 us (19%)
  matrix products  28.3 us (8%)
  between operations  14.2 us (4%)
  local copies, waits for them, and re-layouts  4.05 us (1%)
    psum x1, blocking collectives, shards(): total = lax.psum(partial_value, 'elem')  119 us
    reduce_scatter x1, waiting for transfers between devices, shards(): lax.psum_scatter(terms_blocks(slope_x, slope_y, q_re, q_im, lattice_x, co...  66.2 us
    all_gather x1, blocking collectives, shards(): whole = lax.all_gather(phasors, 'pts', axis=2, tiled=True)  41.7 us
    cos x4, other arithmetic, partial_field(): left = jnp.concatenate([jnp.cos(beam_y), jnp.sin(beam_y)], 1)  29.4 us
    cos x4, other arithmetic, surface_terms(): left = jnp.concatenate([jnp.cos(beam_y), jnp.sin(beam_y)], 1)  29.4 us
    dot_general x4, matrix products, partial_field(): jnp.dot(left, right, precision=HIGH, preferred_element_type=jnp.float32)  16.9 us
    dot_general x4, matrix products, surface_terms(): lax.dot_general(left, right, (((0,), (0,)), ((), ())), precision=HIGH, pr...  11.4 us
  transfers between devices with their start and end apart: 1, of which 1 were waited for; matrix products, arithmetic and copies ran while one was open for 0% of the time, Pallas kernels for 0%

commit v1 on v0

--- a/solution.py
+++ b/solution.py
@@ -118,7 +118,9 @@
     whole = lax.all_gather(phasors, "pts", axis=2, tiled=True)
     lattice_y = jnp.arange(NY_EL).astype(jnp.float32) - (NY_EL - 1) / 2.0
     partial_value = field_blocks(slope_x, slope_y, lattice_x, lattice_y, whole[0], whole[1])
-    total = lax.psum(partial_value, "elem")
+    total = partial_value
+    for hop in (1, 2, 4, 8, 16):
+        total = total + lax.ppermute(total, "elem", [(dev, dev ^ hop) for dev in range(32)])
     field = direct + scale[None, :] * total
     q_re, q_im = weights(field, scale, noise)
     cols_here = jnp.arange(cols_dev * lax.axis_size("pts")).astype(jnp.float32) - (NY_EL - 1) / 2.0

time: 338 us -> 247 us (0.73)
  blocking collectives: 161 us -> 41.7 us
  starting transfers between devices: 0.04 us -> 17 us
  waiting for transfers between devices: 66.2 us -> 77.9 us
    psum x1 -> x0, blocking collectives: 119 us -> none  [shards(): total = lax.psum(partial_value, 'elem')]
    ppermute x0 -> x5, starting transfers between devices: none -> 17 us  [shards(): lax.ppermute(total, 'elem', [(dev, dev ^ hop) for dev in range(32)])]
    ppermute x0 -> x5, waiting for transfers between devices: none -> 11.6 us  [shards(): lax.ppermute(total, 'elem', [(dev, dev ^ hop) for dev in range(32)])]
  transfers between devices with their start and end apart: 1 -> 6, of which waited for: 1 -> 6; matrix products, arithmetic and copies ran while one was open for 0% -> 0% of each run, Pallas kernels for 0% -> 0%
where the time goes in v1:
time: 247 us
  waiting for transfers between devices  77.9 us (32%)
  other arithmetic  63.5 us (26%)
  blocking collectives  41.7 us (17%)
  matrix products  28.3 us (11%)
  starting transfers between devices  17 us (7%)
  between operations  14.3 us (6%)
  local copies, waits for them, and re-layouts  4.04 us (2%)
    reduce_scatter x1, waiting for transfers between devices, shards(): lax.psum_scatter(terms_blocks(slope_x, slope_y, q_re, q_im, lattice_x, co...  66.3 us
    all_gather x1, blocking collectives, shards(): whole = lax.all_gather(phasors, 'pts', axis=2, tiled=True)  41.7 us
    cos x4, other arithmetic, surface_terms(): left = jnp.concatenate([jnp.cos(beam_y), jnp.sin(beam_y)], 1)  29.4 us
    cos x4, other arithmetic, partial_field(): left = jnp.concatenate([jnp.cos(beam_y), jnp.sin(beam_y)], 1)  29.4 us
    ppermute x5, starting transfers between devices, shards(): lax.ppermute(total, 'elem', [(dev, dev ^ hop) for dev in range(32)])  17 us
    dot_general x4, matrix products, partial_field(): jnp.dot(left, right, precision=HIGH, preferred_element_type=jnp.float32)  16.9 us
    ppermute x5, waiting for transfers between devices, shards(): lax.ppermute(total, 'elem', [(dev, dev ^ hop) for dev in range(32)])  11.6 us
    dot_general x4, matrix products, surface_terms(): lax.dot_general(left, right, (((0,), (0,)), ((), ())), precision=HIGH, pr...  11.4 us
  transfers between devices with their start and end apart: 6, of which 6 were waited for; matrix products, arithmetic and copies ran while one was open for 0% of the time, Pallas kernels for 0%

profile of v1, /device:TPU:2, one launch (start us, length us, event | category | flops | bytes accessed | tf_op | source)
XLA Modules:
  0.0 247.1 jit_solution(7936981296764045781)
XLA Ops:
  7.2 0.8 copy.18
  8.0 0.1 fusion.39
  8.3 41.7 %all_gather.3 = f32[2,32,1024]{1,0,2:T(2,128)S(1)} all-gather(f32[2,32,64]{1,0,2:T(2,128)S(1)} %pad_maximum_fusion), channel_id=1, replica_groups=mesh['pts'=16,'elem'=32] {'pts'}, dimensions={2}, use_global_device_ids=true | all-gather | bytes 278528 | tf_op jit(solution)/shard_map/all_gather | solution.py:118
  49.9 0.8 fusion.38
  50.9 0.3 maximum_maximum_fusion
  51.3 47.9 %while.24 = (s32[]{:T(128)}, f32[4,2,512]{2,1,0:T(2,128)S(1)}, f32[4,512]{1,0:T(4,128)S(1)}, f32[32]{0:T(128)S(1)}, f32[4,512]{1,0:T(4,128)S(1)}, /*index=5*/f32[2048,64]{1,0:T(8,128)S(1)}, s32[]{:T(128)}) while((s32[]{:T(128)}, f32[4,2,512]{2,1,0:T(2,128)S(1)}, f32[4,512]{1,0:T(4,128)S(1)}, f32[32]{0:T(128)S(1)}, ...), condition=%wide.region_3.4_spmd.clone, body=%wide.region_0.3_spmd.clone.sunk | while | flops 807029760 | bytes 9208021 | solution.py:74
  51.3 7.3 %multiply_cosine_fusion.6 = (f32[512,1024]{1,0:T(8,128)S(1)}, f32[512,1024]{1,0:T(8,128)S(1)}) fusion(f32[1024]{0:T(1024)S(1)} %convert_add_fusion.5, f32[512]{0:T(512)S(1)} %bitcast.76), kind=kLoop, calls=%fused_computation.7.clone.1 | loop fusion | flops 524288 | bytes 4200448 | tf_op jit(solution)/shard_map/while/body/eval_jaxpr/cos | solution.py:21
  58.7 4.2 %fusion.52 = f32[512,64]{0,1:T(8,128)S(1)} fusion(f32[2048,64]{1,0:T(8,128)S(1)} %get-tuple-element.375, f32[512,1024]{1,0:T(8,128)S(1)} %get-tuple-element.334, f32[512,1024]{1,0:T(8,128)S(1)} %get-tuple-element.335), kind=kOutput, calls=%fused_computation.2.clone.1 | convolution fusion | flops 806354944 | bytes 4849664 | tf_op jit(solution)/shard_map/while/body/eval_jaxpr/dot_general | solution.py:29
  62.9 0.3 fusion.53
  63.3 7.3 %multiply_cosine_fusion.6 = (f32[512,1024]{1,0:T(8,128)S(1)}, f32[512,1024]{1,0:T(8,128)S(1)}) fusion(f32[1024]{0:T(1024)S(1)} %convert_add_fusion.5, f32[512]{0:T(512)S(1)} %bitcast.76), kind=kLoop, calls=%fused_computation.7.clone.1 | loop fusion | flops 524288 | bytes 4200448 | tf_op jit(solution)/shard_map/while/body/eval_jaxpr/cos | solution.py:21
  70.6 4.2 %fusion.52 = f32[512,64]{0,1:T(8,128)S(1)} fusion(f32[2048,64]{1,0:T(8,128)S(1)} %get-tuple-element.375, f32[512,1024]{1,0:T(8,128)S(1)} %get-tuple-element.334, f32[512,1024]{1,0:T(8,128)S(1)} %get-tuple-element.335), kind=kOutput, calls=%fused_computation.2.clone.1 | convolution fusion | flops 806354944 | bytes 4849664 | tf_op jit(solution)/shard_map/while/body/eval_jaxpr/dot_general | solution.py:29
  74.8 0.3 fusion.53
  75.2 7.3 %multiply_cosine_fusion.6 = (f32[512,1024]{1,0:T(8,128)S(1)}, f32[512,1024]{1,0:T(8,128)S(1)}) fusion(f32[1024]{0:T(1024)S(1)} %convert_add_fusion.5, f32[512]{0:T(512)S(1)} %bitcast.76), kind=kLoop, calls=%fused_computation.7.clone.1 | loop fusion | flops 524288 | bytes 4200448 | tf_op jit(solution)/shard_map/while/body/eval_jaxpr/cos | solution.py:21
  82.6 4.2 %fusion.52 = f32[512,64]{0,1:T(8,128)S(1)} fusion(f32[2048,64]{1,0:T(8,128)S(1)} %get-tuple-element.375, f32[512,1024]{1,0:T(8,128)S(1)} %get-tuple-element.334, f32[512,1024]{1,0:T(8,128)S(1)} %get-tuple-element.335), kind=kOutput, calls=%fused_computation.2.clone.1 | convolution fusion | flops 806354944 | bytes 4849664 | tf_op jit(solution)/shard_map/while/body/eval_jaxpr/dot_general | solution.py:29
  86.8 0.3 fusion.53
  87.2 7.3 %multiply_cosine_fusion.6 = (f32[512,1024]{1,0:T(8,128)S(1)}, f32[512,1024]{1,0:T(8,128)S(1)}) fusion(f32[1024]{0:T(1024)S(1)} %convert_add_fusion.5, f32[512]{0:T(512)S(1)} %bitcast.76), kind=kLoop, calls=%fused_computation.7.clone.1 | loop fusion | flops 524288 | bytes 4200448 | tf_op jit(solution)/shard_map/while/body/eval_jaxpr/cos | solution.py:21
  94.6 4.2 %fusion.52 = f32[512,64]{0,1:T(8,128)S(1)} fusion(f32[2048,64]{1,0:T(8,128)S(1)} %get-tuple-element.375, f32[512,1024]{1,0:T(8,128)S(1)} %get-tuple-element.334, f32[512,1024]{1,0:T(8,128)S(1)} %get-tuple-element.335), kind=kOutput, calls=%fused_computation.2.clone.1 | convolution fusion | flops 806354944 | bytes 4849664 | tf_op jit(solution)/shard_map/while/body/eval_jaxpr/dot_general | solution.py:29
  98.8 0.3 fusion.53
  99.2 1.9 collective-permute-start
  101.1 1.1 collective-permute-done
  102.3 2.4 collective-permute-start.1
  104.7 3.2 %collective-permute-done.1 = f32[2,2048]{1,0:T(2,128)S(1)} collective-permute-done((f32[2,2048]{1,0:T(2,128)S(1)}, f32[2,2048]{1,0:T(2,128)S(1)}, u32[]{:S(2)}, u32[]{:S(2)}) %collective-permute-start.1) | collective-permute-done | bytes 16416 | tf_op jit(solution)/shard_map/ppermute | solution.py:123
  107.9 4.0 %collective-permute-start.2 = (f32[2,2048]{1,0:T(2,128)S(1)}, f32[2,2048]{1,0:T(2,128)S(1)}, u32[]{:S(2)}, u32[]{:S(2)}) collective-permute-start(f32[2,2048]{1,0:T(2,128)S(1)} %add.68), channel_id=1, source_target_pairs={{0,4},{1,5},{2,6},{3,7},{4,0},{5,1},{6,2},{7,3},{8,12},{9,13},{10,... | collective-permute-start | bytes 49160 | tf_op jit(solution)/shard_map/ppermute | solution.py:123
  111.9 3.1 %collective-permute-done.2 = f32[2,2048]{1,0:T(2,128)S(1)} collective-permute-done((f32[2,2048]{1,0:T(2,128)S(1)}, f32[2,2048]{1,0:T(2,128)S(1)}, u32[]{:S(2)}, u32[]{:S(2)}) %collective-permute-start.2) | collective-permute-done | bytes 16416 | tf_op jit(solution)/shard_map/ppermute | solution.py:123
  115.1 3.5 %collective-permute-start.3 = (f32[2,2048]{1,0:T(2,128)S(1)}, f32[2,2048]{1,0:T(2,128)S(1)}, u32[]{:S(2)}, u32[]{:S(2)}) collective-permute-start(f32[2,2048]{1,0:T(2,128)S(1)} %add.69), channel_id=1, source_target_pairs={{0,8},{1,9},{2,10},{3,11},{4,12},{5,13},{6,14},{7,15},{8,0},{9,1},... | collective-permute-start | bytes 49160 | tf_op jit(solution)/shard_map/ppermute | solution.py:123
  118.5 2.1 collective-permute-done.3
  120.7 5.1 %collective-permute-start.4 = (f32[2,2048]{1,0:T(2,128)S(1)}, f32[2,2048]{1,0:T(2,128)S(1)}, u32[]{:S(2)}, u32[]{:S(2)}) collective-permute-start(f32[2,2048]{1,0:T(2,128)S(1)} %add.70), channel_id=1, source_target_pairs={{0,16},{1,17},{2,18},{3,19},{4,20},{5,21},{6,22},{7,23},{8,24},{9,... | collective-permute-start | bytes 49160 | tf_op jit(solution)/shard_map/ppermute | solution.py:123
  125.8 2.0 collective-permute-done.4
  128.0 0.5 copy-done
  128.5 42.9 %while.25 = (s32[]{:T(128)}, f32[1024,64]{0,1:T(8,128)S(1)}, f32[4,512]{1,0:T(4,128)S(1)}, f32[4,512]{1,0:T(4,128)S(1)}, f32[4,512]{1,0:T(4,128)S(1)}, /*index=5...) while((s32[]{:T(128)}, f32[1024,64]{0,1:T(8,128)S(1)}, f32[4,512]{1,0:T(4,128)S(1)}, ...), condition=%wide.region_5.6_spmd.clone, body=%wide.region_4.5_spmd.clone.sunk | while | flops 807291904 | bytes 10780911 | solution.py:95
  128.5 0.3 fusion.57
  128.8 7.3 %multiply_cosine_fusion.7 = (f32[512,1024]{1,0:T(8,128)S(1)}, f32[512,1024]{1,0:T(8,128)S(1)}) fusion(f32[1024]{0:T(1024)S(1)} %convert_add_fusion.6, f32[512]{0:T(512)S(1)} %bitcast.72), kind=kLoop, calls=%fused_computation.29.clone.1 | loop fusion | flops 524288 | bytes 4200448 | tf_op jit(solution)/shard_map/while/body/eval_jaxpr/cos | solution.py:51
  136.2 2.8 %fusion.58 = f32[2048,64]{0,1:T(8,128)S(1)} fusion(f32[512,1024]{1,0:T(8,128)S(1)} %get-tuple-element.347, f32[512,1024]{1,0:T(8,128)S(1)} %get-tuple-element.348, f32[512,32]{0,1:T(8,128)S(1)} %get-tuple-element.352, f32[512,32]{0,1:T(8,128)S(1)} %get-tuple-element.353), kind=kOutput, calls=%fused_computation.24.clone.1 | convolution fusion | flops 806387712 | bytes 4849664 | tf_op jit(solution)/shard_map/while/body/eval_jaxpr/dot_general | solution.py:53
  139.1 0.1 maximum_add_fusion.2
  139.2 0.3 fusion.57
  139.6 7.3 %multiply_cosine_fusion.7 = (f32[512,1024]{1,0:T(8,128)S(1)}, f32[512,1024]{1,0:T(8,128)S(1)}) fusion(f32[1024]{0:T(1024)S(1)} %convert_add_fusion.6, f32[512]{0:T(512)S(1)} %bitcast.72), kind=kLoop, calls=%fused_computation.29.clone.1 | loop fusion | flops 524288 | bytes 4200448 | tf_op jit(solution)/shard_map/while/body/eval_jaxpr/cos | solution.py:51
  146.9 2.8 %fusion.58 = f32[2048,64]{0,1:T(8,128)S(1)} fusion(f32[512,1024]{1,0:T(8,128)S(1)} %get-tuple-element.347, f32[512,1024]{1,0:T(8,128)S(1)} %get-tuple-element.348, f32[512,32]{0,1:T(8,128)S(1)} %get-tuple-element.352, f32[512,32]{0,1:T(8,128)S(1)} %get-tuple-element.353), kind=kOutput, calls=%fused_computation.24.clone.1 | convolution fusion | flops 806387712 | bytes 4849664 | tf_op jit(solution)/shard_map/while/body/eval_jaxpr/dot_general | solution.py:53
  149.8 0.1 maximum_add_fusion.2
  149.9 0.3 fusion.57
  150.3 7.3 %multiply_cosine_fusion.7 = (f32[512,1024]{1,0:T(8,128)S(1)}, f32[512,1024]{1,0:T(8,128)S(1)}) fusion(f32[1024]{0:T(1024)S(1)} %convert_add_fusion.6, f32[512]{0:T(512)S(1)} %bitcast.72), kind=kLoop, calls=%fused_computation.29.clone.1 | loop fusion | flops 524288 | bytes 4200448 | tf_op jit(solution)/shard_map/while/body/eval_jaxpr/cos | solution.py:51
  157.6 2.8 %fusion.58 = f32[2048,64]{0,1:T(8,128)S(1)} fusion(f32[512,1024]{1,0:T(8,128)S(1)} %get-tuple-element.347, f32[512,1024]{1,0:T(8,128)S(1)} %get-tuple-element.348, f32[512,32]{0,1:T(8,128)S(1)} %get-tuple-element.352, f32[512,32]{0,1:T(8,128)S(1)} %get-tuple-element.353), kind=kOutput, calls=%fused_computation.24.clone.1 | convolution fusion | flops 806387712 | bytes 4849664 | tf_op jit(solution)/shard_map/while/body/eval_jaxpr/dot_general | solution.py:53
  160.7 0.3 fusion.57
  161.0 7.3 %multiply_cosine_fusion.7 = (f32[512,1024]{1,0:T(8,128)S(1)}, f32[512,1024]{1,0:T(8,128)S(1)}) fusion(f32[1024]{0:T(1024)S(1)} %convert_add_fusion.6, f32[512]{0:T(512)S(1)} %bitcast.72), kind=kLoop, calls=%fused_computation.29.clone.1 | loop fusion | flops 524288 | bytes 4200448 | tf_op jit(solution)/shard_map/while/body/eval_jaxpr/cos | solution.py:51
  168.4 2.8 %fusion.58 = f32[2048,64]{0,1:T(8,128)S(1)} fusion(f32[512,1024]{1,0:T(8,128)S(1)} %get-tuple-element.347, f32[512,1024]{1,0:T(8,128)S(1)} %get-tuple-element.348, f32[512,32]{0,1:T(8,128)S(1)} %get-tuple-element.352, f32[512,32]{0,1:T(8,128)S(1)} %get-tuple-element.353), kind=kOutput, calls=%fused_computation.24.clone.1 | convolution fusion | flops 806387712 | bytes 4849664 | tf_op jit(solution)/shard_map/while/body/eval_jaxpr/dot_general | solution.py:53
  171.3 1.0 copy.26
  172.4 66.3 %reduce-scatter.4.cloned.1.call-done = f32[64,64]{1,0:T(8,128)} async-done(((f32[1024,64]{1,0:T(8,128)}), f32[64,64]{1,0:T(8,128)}) %reduce-scatter.4.cloned.1.call-update) | async-done | bytes 16400 | tf_op jit(solution)/shard_map/reduce_scatter | solution.py:127
  238.6 0.9 fusion.34
  239.5 0.7 copy.25
  (60 shorter events, 0.9 us)
Async XLA Ops:
  7.2 231.5 %reduce-scatter.4.cloned.1.call-start = ((), (), s32[]{:S(2)}) async-start(), calls=%async_computation.1 | async-start | bytes 557056 | tf_op jit(solution)/shard_map/reduce_scatter | solution.py:127
  8.2 42.6 %copy-start.2 = (s32[2048]{0:T(1024)S(1)}, s32[2048]{0:T(1024)}, u32[]{:S(2)}) copy-start(s32[2048]{0:T(1024)} %param.13) | copy-start | bytes 24580
  8.2 42.6 %copy-start.3 = (s32[2048]{0:T(1024)S(1)}, s32[2048]{0:T(1024)}, u32[]{:S(2)}) copy-start(s32[2048]{0:T(1024)} %param.12) | copy-start | bytes 24580
  8.3 42.6 %copy-start.5 = (s32[32]{0:T(128)S(1)}, s32[32]{0:T(128)}, u32[]{:S(2)}) copy-start(s32[32]{0:T(128)} %param.11) | copy-start | bytes 388
  51.2 76.6 %copy-start.1 = (f32[2,2048]{1,0:T(2,128)S(1)}, f32[2,2048]{1,0:T(2,128)}, u32[]{:S(2)}) copy-start(f32[2,2048]{1,0:T(2,128)} %param.14) | copy-start | bytes 49156
  51.2 76.7 %copy-start.4 = (f32[2048]{0:T(1024)S(1)}, f32[2048]{0:T(1024)}, u32[]{:S(2)}) copy-start(f32[2048]{0:T(1024)} %param.15) | copy-start | bytes 24580
  99.2 3.1 %collective-permute-start = (f32[2,2048]{1,0:T(2,128)S(1)}, f32[2,2048]{1,0:T(2,128)S(1)}, u32[]{:S(2)}, u32[]{:S(2)}) collective-permute-start(f32[2,2048]{1,0:T(2,128)S(1)} %bitcast.82), channel_id=1, source_target_pairs={{0,1},{1,0},{2,3},{3,2},{4,5},{5,4},{6,7},{7,6},{8,9},{9,8},{10,11... | collective-permute-start | bytes 49160 | tf_op jit(solution)/shard_map/ppermute | solution.py:123
  102.3 5.6 %collective-permute-start.1 = (f32[2,2048]{1,0:T(2,128)S(1)}, f32[2,2048]{1,0:T(2,128)S(1)}, u32[]{:S(2)}, u32[]{:S(2)}) collective-permute-start(f32[2,2048]{1,0:T(2,128)S(1)} %add.67), channel_id=1, source_target_pairs={{0,2},{1,3},{2,0},{3,1},{4,6},{5,7},{6,4},{7,5},{8,10},{9,11},{10,... | collective-permute-start | bytes 49160 | tf_op jit(solution)/shard_map/ppermute | solution.py:123
  107.9 7.1 %collective-permute-start.2 = (f32[2,2048]{1,0:T(2,128)S(1)}, f32[2,2048]{1,0:T(2,128)S(1)}, u32[]{:S(2)}, u32[]{:S(2)}) collective-permute-start(f32[2,2048]{1,0:T(2,128)S(1)} %add.68), channel_id=1, source_target_pairs={{0,4},{1,5},{2,6},{3,7},{4,0},{5,1},{6,2},{7,3},{8,12},{9,13},{10,... | collective-permute-start | bytes 49160 | tf_op jit(solution)/shard_map/ppermute | solution.py:123
  115.1 5.6 %collective-permute-start.3 = (f32[2,2048]{1,0:T(2,128)S(1)}, f32[2,2048]{1,0:T(2,128)S(1)}, u32[]{:S(2)}, u32[]{:S(2)}) collective-permute-start(f32[2,2048]{1,0:T(2,128)S(1)} %add.69), channel_id=1, source_target_pairs={{0,8},{1,9},{2,10},{3,11},{4,12},{5,13},{6,14},{7,15},{8,0},{9,1},... | collective-permute-start | bytes 49160 | tf_op jit(solution)/shard_map/ppermute | solution.py:123
  120.7 7.1 %collective-permute-start.4 = (f32[2,2048]{1,0:T(2,128)S(1)}, f32[2,2048]{1,0:T(2,128)S(1)}, u32[]{:S(2)}, u32[]{:S(2)}) collective-permute-start(f32[2,2048]{1,0:T(2,128)S(1)} %add.70), channel_id=1, source_target_pairs={{0,16},{1,17},{2,18},{3,19},{4,20},{5,21},{6,22},{7,23},{8,24},{9,... | collective-permute-start | bytes 49160 | tf_op jit(solution)/shard_map/ppermute | solution.py:123
  127.9 0.6 copy-start
Sparse Core Ops, SparseCore 0:
  172.5 66.1 reduce-scatter.3
